TPU v7x, 128 devices: a whole 4x4x4 slice. The times are simulated.
128 devices in a mesh: rows: 8 (over x, core), cols: 16 (over y, z).
Axes of the slice: x: 4, y: 4, z: 4, core: 2. Of those that a mesh axis runs over, the one named last changes fastest.
Arguments:
- cells: int32 [1024], replicated, may hold values from 0 to 65535, as said below
- gram_slots: float32 [6, 4096, 2048], P(None, 'rows', 'cols'), may hold values from -6 to 6
- diag_inverse: float32 [2, 4096, 4096], P(None, 'rows', 'cols'), may hold values from -1 to 2.1, as said below
- lower_block: float32 [4096, 4096], P('rows', 'cols'), may hold values from -0.09375 to 0.09375
- trail_factor: float32 [4, 2, 4096, 4096], P(None, None, 'rows', 'cols'), may hold values from -0.0625 to 0.0625
Outputs:
- y_panels: float32 [2, 4096, 1024], P(None, 'rows')
- g_trail: float32 [4, 4096, 1024], P(None, 'rows', 'cols')
Inputs may be any that keep to these rules, and one draw needn't show every extreme that they name: Within each aligned run of 64 list positions no column block owns more than 8 cells; one column block owns exactly 8 in every run, and so 128 listed cells in all, and no column block owns more than 128. `diag_inverse`: each matrix is lower triangular with a positive diagonal.
All inputs are finite; a program needn't handle non-finite values.
Results may differ from a plain program's by a relative error of at most 0.00011.
Values sent between devices are 32-bit elements; how exact they have to be, the bound alone decides.
No kernel may reach another device: no remote copies, remote signals or barrier semaphores. Data moves between devices by JAX's collectives and lax.ppermute only.
A program may use at most 128 MiB of HBM per device.

v0:
```python
import jax
import jax.numpy as jnp
from jax import lax
from jax.sharding import PartitionSpec as P

NCELL = 65536


def from_root(value, axis, source):
    kept = jnp.where(lax.axis_index(axis) == source, value, 0).astype(value.dtype)
    return lax.psum(kept, axis)


def body(cells, gram_slots, diag_inverse, lower_block, trail_factor):
    highest = lax.Precision.HIGHEST
    col_count = lax.axis_size("cols")
    row_count = lax.axis_size("rows")
    col_index = lax.axis_index("cols")
    col_rows = diag_inverse.shape[2]
    spread_ratio = col_count // row_count
    list_len = cells.shape[0]
    block_len = list_len // col_count
    capacity = gram_slots.shape[2]
    bound_pair = capacity // col_count
    owners = cells // (NCELL // col_count)
    onehot = (owners[:, None] == jnp.arange(col_count, dtype=jnp.int32)[None, :]).astype(jnp.int32)
    slots_of = jnp.sum((jnp.cumsum(onehot, axis=0) - onehot) * onehot, axis=1)
    blocked = onehot.reshape(col_count, block_len, col_count)
    pair_rank = jnp.sum((jnp.cumsum(blocked, axis=1) - blocked) * blocked, axis=2).reshape(list_len)
    is_mine = owners == col_index
    panel_slots = gram_slots[0:2]
    whole = lax.all_gather(panel_slots, "cols", axis=2, tiled=True)
    panel_rhs = jnp.take(whole, owners * capacity + slots_of, axis=2)
    position = jnp.arange(list_len, dtype=jnp.int32) // block_len * bound_pair + pair_rank
    matches = (position[:, None] == jnp.arange(capacity, dtype=jnp.int32)[None, :]) & is_mine[
        :, None
    ]
    send_index = jnp.sum(jnp.where(matches, slots_of[:, None], 0), axis=0)
    outgoing = jnp.take(gram_slots[2:], send_index, axis=2)
    incoming = lax.all_to_all(outgoing, "cols", split_axis=2, concat_axis=2, tiled=True)
    mine_owner = lax.dynamic_slice_in_dim(owners, col_index * block_len, block_len)
    mine_rank = lax.dynamic_slice_in_dim(pair_rank, col_index * block_len, block_len)
    trail_rhs = jnp.take(incoming, mine_owner * bound_pair + mine_rank, axis=2)

    def to_columns(block):
        start = col_index % spread_ratio * col_rows
        piece = lax.dynamic_slice_in_dim(block, start, col_rows, 0)
        return from_root(piece, "rows", col_index // spread_ratio)

    def solve_panel(inverse, rhs_rows):
        partial_sum = jnp.dot(
            inverse, to_columns(rhs_rows), precision=highest, preferred_element_type=jnp.float32
        )
        return lax.psum(partial_sum, "cols")

    first_panel = solve_panel(diag_inverse[0], panel_rhs[0])
    first_rows = to_columns(first_panel)
    lower_term = jnp.dot(
        lower_block, first_rows, precision=highest, preferred_element_type=jnp.float32
    )
    first_trail = jnp.einsum(
        "trc,ck->trk",
        trail_factor[:, 0],
        first_rows,
        precision=highest,
        preferred_element_type=jnp.float32,
    )
    trail_rhs = trail_rhs - lax.psum_scatter(first_trail, "cols", scatter_dimension=2, tiled=True)
    second_rhs = panel_rhs[1] - lax.psum(lower_term, "cols")
    second_panel = solve_panel(diag_inverse[1], second_rhs)
    second_rows = to_columns(second_panel)
    second_trail = jnp.einsum(
        "trc,ck->trk",
        trail_factor[:, 1],
        second_rows,
        precision=highest,
        preferred_element_type=jnp.float32,
    )
    trail_out = trail_rhs - lax.psum_scatter(second_trail, "cols", scatter_dimension=2, tiled=True)
    return (jnp.stack([first_panel, second_panel]), trail_out)


def solution(mesh):
    return jax.shard_map(
        body,
        mesh=mesh,
        in_specs=(
            P(),
            P(None, "rows", "cols"),
            P(None, "rows", "cols"),
            P("rows", "cols"),
            P(None, None, "rows", "cols"),
        ),
        out_specs=(P(None, "rows", None), P(None, "rows", "cols")),
        check_vma=False,
    )
```

profile of v0, /device:TPU:0, one launch (start us, length us, event | category | flops | bytes accessed | tf_op | source)
XLA Modules:
  0.0 838.1 jit_solution(15641195324254651061)
XLA Ops:
  7.2 0.0 all-gather.2.cloned.1.call-start
  7.2 1.1 slice.32
  8.4 1.0 copy.54
  9.4 0.0 all-gather.2.cloned.1.call-update
  9.4 0.0 all-reduce.8.cloned.1.call-start
  9.4 0.7 broadcast_compare_fusion
  10.2 4.5 reduce-window.6
  14.7 0.1 slice.46
  14.8 0.1 copy.43
  14.9 0.1 copy.44
  15.0 0.1 broadcast_add_fusion
  15.2 68.9 %all-gather.2.cloned.1.call-done = f32[2,512,2048]{1,0,2:T(2,128)} async-done(((f32[2,512,128]{1,0,2:T(2,128)}), f32[2,512,2048]{1,0,2:T(2,128)}) %all-gather.2.cloned.1.call-update) | async-done | bytes 8388624 | tf_op jit(solution)/shard_map/all_gather | solution.py:32
  84.1 14.9 %gather_fusion = f32[1024,2,512]{2,1,0:T(2,128)} fusion(f32[2,512,2048]{1,0,2:T(2,128)} %all-gather.2.cloned.1.call-done, s32[1024]{0:T(1024)S(1)} %broadcast_clamp_fusion), kind=kCustom, calls=%fused_computation | custom fusion | bytes 8392704 | tf_op jit(solution)/shard_map/jit(_take)/gather | solution.py:33
  99.0 3.0 fusion
  102.0 0.4 slice_bitcast_fusion
  102.5 1.1 select_bitcast_fusion.1
  103.6 0.0 all-reduce.10.cloned.1.call-start
  103.6 62.0 %all-reduce.8.cloned.1.call-done = f32[256,1024]{0,1:T(8,128)} async-done(((f32[256,1024]{0,1:T(8,128)}), f32[256,1024]{0,1:T(8,128)}) %all-reduce.8.cloned.1.call-update) | async-done | bytes 1048592 | tf_op jit(solution)/shard_map/psum | solution.py:11
  165.7 4.5 convolution_bitcast_fusion.4
  170.2 0.0 all-reduce.10.cloned.1.call-update
  170.2 0.0 all-reduce.12.cloned.1.call-start
  170.3 89.9 %all-reduce.10.cloned.1.call-done = f32[512,1024]{0,1:T(8,128)} async-done(((f32[512,1024]{0,1:T(8,128)}), f32[512,1024]{0,1:T(8,128)}) %all-reduce.10.cloned.1.call-update) | async-done | bytes 2097168 | tf_op jit(solution)/shard_map/psum | solution.py:54
  260.1 2.3 dynamic-slice_select_fusion.1
  262.4 0.0 all-reduce.12.cloned.1.call-update
  262.4 0.0 all-reduce.14.cloned.1.call-start
  262.5 62.2 %all-reduce.12.cloned.1.call-done = f32[256,1024]{0,1:T(8,128)} async-done(((f32[256,1024]{0,1:T(8,128)}), f32[256,1024]{0,1:T(8,128)}) %all-reduce.12.cloned.1.call-update) | async-done | bytes 1048592 | tf_op jit(solution)/shard_map/psum | solution.py:11
  324.7 4.4 convolution_bitcast_fusion.3
  329.1 0.0 all-reduce.14.cloned.1.call-update
  329.1 0.0 all-reduce.16.cloned.1.call-start
  329.2 89.9 %all-reduce.14.cloned.1.call-done = f32[512,1024]{0,1:T(8,128)} async-done(((f32[512,1024]{0,1:T(8,128)}), f32[512,1024]{0,1:T(8,128)}) %all-reduce.14.cloned.1.call-update) | async-done | bytes 2097168 | tf_op jit(solution)/shard_map/psum | solution.py:69
  419.0 2.4 fusion.5
  421.5 0.0 all-reduce.18.cloned.1.call-start
  421.5 62.0 %all-reduce.16.cloned.1.call-done = f32[256,1024]{0,1:T(8,128)} async-done(((f32[256,1024]{0,1:T(8,128)}), f32[256,1024]{0,1:T(8,128)}) %all-reduce.16.cloned.1.call-update) | async-done | bytes 1048592 | tf_op jit(solution)/shard_map/psum | solution.py:11
  483.5 4.5 convolution_bitcast_fusion.2
  488.0 0.0 all-reduce.18.cloned.1.call-update
  488.0 0.0 all-reduce.20.cloned.1.call-start
  488.1 89.9 %all-reduce.18.cloned.1.call-done = f32[512,1024]{0,1:T(8,128)} async-done(((f32[512,1024]{0,1:T(8,128)}), f32[512,1024]{0,1:T(8,128)}) %all-reduce.18.cloned.1.call-update) | async-done | bytes 2097168 | tf_op jit(solution)/shard_map/psum | solution.py:54
  577.9 2.3 dynamic-slice_select_fusion
  580.2 0.0 all-reduce.20.cloned.1.call-update
  580.2 0.2 reduce-scatter.3.cloned.1.call-start
  580.5 10.3 %convolution_bitcast_fusion.1 = f32[4,512,1024]{1,2,0:T(8,128)} fusion(f32[4,2,512,256]{3,2,1,0:T(8,128)} %param.9, f32[256,1024]{0,1:T(8,128)S(1)} %copy-done.3), kind=kOutput, calls=%fused_computation.7 | convolution fusion | flops 6442450944 | bytes 11534336 | tf_op jit(solution)/shard_map/trc,ck->trk/dot_general | solution.py:61
  590.8 0.0 reduce-scatter.3.cloned.1.call-update
  590.8 0.0 reduce-scatter.5.cloned.1.call-start
  590.9 51.8 %all-reduce.20.cloned.1.call-done = f32[256,1024]{0,1:T(8,128)} async-done(((f32[256,1024]{0,1:T(8,128)}), f32[256,1024]{0,1:T(8,128)}) %all-reduce.20.cloned.1.call-update) | async-done | bytes 1048592 | tf_op jit(solution)/shard_map/psum | solution.py:11
  642.6 10.6 %convolution_bitcast_fusion = f32[4,512,1024]{1,2,0:T(8,128)} fusion(f32[4,2,512,256]{3,2,1,0:T(8,128)} %param.9, f32[256,1024]{0,1:T(8,128)} %all-reduce.20.cloned.1.call-done), kind=kOutput, calls=%fused_computation.6 | convolution fusion | flops 6442450944 | bytes 11534336 | tf_op jit(solution)/shard_map/trc,ck->trk/dot_general | solution.py:72
  653.2 0.0 reduce-scatter.5.cloned.1.call-update
  653.2 0.1 eq.70
  653.3 0.1 copy.47
  653.4 1.4 select_reduce_fusion.1
  654.8 0.1 copy.48
  654.9 0.1 reshape.85
  655.0 1.4 copy.55
  656.4 0.8 select_reduce_fusion
  657.2 3.5 gather_fusion.1
  660.7 2.5 select_bitcast_fusion
  663.2 7.0 all-to-all-start
  670.3 0.1 compare_and_fusion.2
  670.4 21.5 %all-to-all-done = f32[4,512,128]{1,0,2:T(4,128)} async-done(((f32[4,512,128]{1,0,2:T(4,128)}), f32[4,512,128]{1,0,2:T(4,128)}, u32[]{:S(2)}, u32[]{:S(2)}) %all-to-all-start) | async-done | bytes 1048608 | tf_op jit(solution)/shard_map/all_to_all | solution.py:40
  691.9 2.1 gather_fusion.2
  694.0 4.0 pad_maximum_fusion
  698.0 5.4 copy.53
  703.4 37.3 %reduce-scatter.3.cloned.1.call-done = f32[4,512,64]{1,2,0:T(8,128)} async-done(((f32[4,512,1024]{1,2,0:T(8,128)}), f32[4,512,64]{1,2,0:T(8,128)}) %reduce-scatter.3.cloned.1.call-update) | async-done | bytes 524304 | tf_op jit(solution)/shard_map/reduce_scatter | solution.py:68
  740.8 88.2 %reduce-scatter.5.cloned.1.call-done = f32[4,512,64]{1,2,0:T(8,128)} async-done(((f32[4,512,1024]{1,2,0:T(8,128)}), f32[4,512,64]{1,2,0:T(8,128)}) %reduce-scatter.5.cloned.1.call-update) | async-done | bytes 524304 | tf_op jit(solution)/shard_map/reduce_scatter | solution.py:79
  829.0 2.2 fusion.12
  (23 shorter events, 0.2 us)
Async XLA Ops:
  7.2 317.5 %copy-start = (f32[512,256]{1,0:T(8,128)S(1)}, f32[512,256]{1,0:T(8,128)}, u32[]{:S(2)}) copy-start(f32[512,256]{1,0:T(8,128)} %param.8) | copy-start | bytes 1572868
  7.2 76.9 %all-gather.2.cloned.1.call-start = ((), (), s32[]{:S(2)}) async-start(), calls=%async_computation.3 | async-start | bytes 8912896 | tf_op jit(solution)/shard_map/all_gather | solution.py:32
  9.4 156.3 %all-reduce.8.cloned.1.call-start = ((), (), s32[]{:S(2)}) async-start(), calls=%async_computation.4 | async-start | bytes 2097152 | tf_op jit(solution)/shard_map/psum | solution.py:11
  103.6 156.5 %all-reduce.10.cloned.1.call-start = ((), (), s32[]{:S(2)}) async-start(), calls=%async_computation.5 | async-start | bytes 4194304 | tf_op jit(solution)/shard_map/psum | solution.py:54
  170.2 154.5 %all-reduce.12.cloned.1.call-start = ((), (), s32[]{:S(2)}) async-start(), calls=%async_computation.6 | async-start | bytes 2097152 | tf_op jit(solution)/shard_map/psum | solution.py:11
  262.4 156.6 %all-reduce.14.cloned.1.call-start = ((), (), s32[]{:S(2)}) async-start(), calls=%async_computation.7 | async-start | bytes 4194304 | tf_op jit(solution)/shard_map/psum | solution.py:69
  329.1 154.4 %all-reduce.16.cloned.1.call-start = ((), (), s32[]{:S(2)}) async-start(), calls=%async_computation.8 | async-start | bytes 2097152 | tf_op jit(solution)/shard_map/psum | solution.py:11
  421.4 159.0 %copy-start.3 = (f32[256,1024]{0,1:T(8,128)S(1)}, f32[256,1024]{0,1:T(8,128)}, u32[]{:S(2)}) copy-start(f32[256,1024]{0,1:T(8,128)} %all-reduce.12.cloned.1.call-done) | copy-start | bytes 3145732
  421.5 156.5 %all-reduce.18.cloned.1.call-start = ((), (), s32[]{:S(2)}) async-start(), calls=%async_computation.9 | async-start | bytes 4194304 | tf_op jit(solution)/shard_map/psum | solution.py:54
  488.0 154.6 %all-reduce.20.cloned.1.call-start = ((), (), s32[]{:S(2)}) async-start(), calls=%async_computation.11 | async-start | bytes 2097152 | tf_op jit(solution)/shard_map/psum | solution.py:11
  580.2 160.5 %reduce-scatter.3.cloned.1.call-start = ((), (), s32[]{:S(2)}) async-start(), calls=%async_computation.10 | async-start | bytes 8912896 | tf_op jit(solution)/shard_map/reduce_scatter | solution.py:68
  590.8 238.2 %reduce-scatter.5.cloned.1.call-start = ((), (), s32[]{:S(2)}) async-start(), calls=%async_computation.12 | async-start | bytes 8912896 | tf_op jit(solution)/shard_map/reduce_scatter | solution.py:79
  653.2 1.8 slice-start
  657.2 36.8 %copy-start.2 = (f32[512,1024]{0,1:T(8,128)S(1)}, f32[512,1024]{0,1:T(8,128)}, u32[]{:S(2)}) copy-start(f32[512,1024]{0,1:T(8,128)} %all-reduce.10.cloned.1.call-done) | copy-start | bytes 6291460
  663.2 28.6 %all-to-all-start = ((f32[4,512,128]{1,0,2:T(4,128)}), f32[4,512,128]{1,0,2:T(4,128)}, u32[]{:S(2)}, u32[]{:S(2)}) async-start(f32[4,512,128]{1,0,2:T(4,128)} %select_bitcast_fusion), calls=%async_computation | async-start | bytes 2097152 | tf_op jit(solution)/shard_map/all_to_all | solution.py:40
  694.0 137.2 %copy-start.1 = (f32[512,256]{1,0:T(8,128)S(1)}, f32[512,256]{1,0:T(8,128)}, u32[]{:S(2)}) copy-start(f32[512,256]{1,0:T(8,128)} %param.8) | copy-start | bytes 1572868
Sparse Core Ops, SparseCore 0:
  10.7 73.3 all-gather.1
  103.7 61.9 all-reduce.7
  170.3 89.7 all-reduce.9
  263.0 61.6 all-reduce.11
  329.2 89.7 all-reduce.13
  421.8 61.6 all-reduce.15
  488.1 89.7 all-reduce.17
  581.0 61.6 all-reduce.19
  646.4 94.2 reduce-scatter.2
  744.4 84.5 reduce-scatter.4
where the time goes:
time: 839 us; the launch traced here: 838 us
  waiting for transfers between devices  724 us (86%)
  matrix products  34.3 us (4%)
  local copies, waits for them, and re-layouts  30.5 us (4%)
  other arithmetic  27.5 us (3%)
  between operations  14.3 us (2%)
    psum x4, waiting for transfers between devices, from_root(): return lax.psum(kept, axis)  238 us
    psum x2, waiting for transfers between devices, solve_panel(): return lax.psum(partial_sum, 'cols')  180 us
    psum x1, waiting for transfers between devices, body(): second_rhs = panel_rhs[1] - lax.psum(lower_term, 'cols')  89.9 us
    reduce_scatter x1, waiting for transfers between devices, body(): lax.psum_scatter(second_trail, 'cols', scatter_dimension=2, tiled=True)  88.2 us
    all_gather x1, waiting for transfers between devices, body(): whole = lax.all_gather(panel_slots, 'cols', axis=2, tiled=True)  68.9 us
    reduce_scatter x1, waiting for transfers between devices, body(): lax.psum_scatter(first_trail, 'cols', scatter_dimension=2, tiled=True)  37.3 us
    all_to_all x1, waiting for transfers between devices, body(): lax.all_to_all(outgoing, 'cols', split_axis=2, concat_axis=2, tiled=True)  21.5 us
  transfers between devices with their start and end apart: 11, of which 11 were waited for; matrix products, arithmetic and copies ran while one was open for 6% of the time, Pallas kernels for 0%

commit v1 on v0

v1 whole, which is shorter than its diff:
```python
import jax
import jax.numpy as jnp
from jax import lax
from jax.sharding import PartitionSpec as P

NCELL = 65536
HIGHEST = lax.Precision.HIGHEST
HIGH = lax.Precision.HIGH
F32 = jnp.float32


def dot(a, b, dims, precision):
    return lax.dot_general(a, b, (dims, ((), ())), precision=precision, preferred_element_type=F32)


def body(cells, gram_slots, diag_inverse, lower_block, trail_factor):
    n_cols = lax.axis_size("cols")
    n_rows = lax.axis_size("rows")
    col = lax.axis_index("cols")
    row = lax.axis_index("rows")
    list_len = cells.shape[0]
    run_len = list_len // n_cols
    slab = list_len // n_rows
    runs_in_slab = slab // run_len
    block_rows = gram_slots.shape[1]
    capacity = gram_slots.shape[2]
    per_run = capacity // n_cols
    slab_slots = runs_in_slab * per_run
    width = diag_inverse.shape[2]
    trail_blocks = trail_factor.shape[0]
    panel_rows = block_rows * n_rows

    owners = cells // (NCELL // n_cols)
    onehot = (owners[:, None] == jnp.arange(n_cols, dtype=jnp.int32)[None, :]).astype(jnp.int32)
    blocked = onehot.reshape(n_cols, run_len, n_cols)
    lower = jnp.tril(jnp.ones((run_len, run_len), F32), -1)
    in_run = jnp.einsum("ij,bjo->bio", lower, blocked.astype(F32)).astype(jnp.int32)
    run_total = jnp.sum(blocked, axis=1)
    before = jnp.sum(
        jnp.where(
            jnp.arange(n_cols)[:, None, None] > jnp.arange(n_cols)[None, :, None],
            run_total[None, :, :],
            0,
        ),
        axis=1,
    )
    pair_rank = jnp.sum(in_run * blocked, axis=2).reshape(list_len)
    slots_of = pair_rank + jnp.sum(before[:, None, :] * blocked, axis=2).reshape(list_len)
    mine = owners == col
    position = jnp.arange(list_len, dtype=jnp.int32) // run_len * per_run + pair_rank
    slot_range = jnp.arange(capacity, dtype=jnp.int32)
    to_list = ((slots_of[None, :] == slot_range[:, None]) & mine[None, :]).astype(F32)
    to_runs = dot(
        ((position[None, :] == slot_range[:, None]) & mine[None, :]).astype(F32),
        to_list,
        ((1,), (1,)),
        lax.Precision.DEFAULT,
    )

    outgoing = lax.dot_general(
        to_runs, gram_slots[0:2], (((1,), (2,)), ((), ())), precision=HIGHEST, preferred_element_type=F32
    )
    outgoing = outgoing.reshape(n_rows, slab_slots, 2, block_rows)
    slab_gram = lax.all_to_all(outgoing, "rows", 0, 0, tiled=True)
    halves = block_rows // width
    first_gram = slab_gram[:, :, 0].reshape(n_rows, slab_slots, halves, width)
    first_gram = first_gram.transpose(0, 2, 1, 3).reshape(n_cols, slab_slots, width)
    first_gram = lax.all_to_all(first_gram, "cols", 0, 0, tiled=True).reshape(n_cols * slab_slots, width)

    slab_owner = lax.dynamic_slice_in_dim(owners, row * slab, slab)
    slab_rank = lax.dynamic_slice_in_dim(pair_rank, row * slab, slab)
    slab_slot = jnp.arange(slab, dtype=jnp.int32) // run_len * per_run + slab_rank
    from_owner = (
        jnp.arange(n_cols * slab_slots, dtype=jnp.int32)[:, None] == (slab_owner * slab_slots + slab_slot)[None, :]
    ).astype(F32)
    own_part = (
        (jnp.arange(slab_slots, dtype=jnp.int32)[:, None] == slab_slot[None, :]) & (slab_owner == col)[None, :]
    ).astype(F32)
    rhs = dot(first_gram, from_owner, ((0,), (0,)), HIGHEST)
    second_gram = lax.dot_general(
        slab_gram[:, :, 1], own_part, (((1,), (0,)), ((), ())), precision=HIGHEST, preferred_element_type=F32
    ).reshape(panel_rows, slab)

    def columns_of(block):
        return lax.all_gather(block, "rows", axis=0, tiled=True)

    inverse_0 = columns_of(diag_inverse[0])
    below = columns_of(lower_block)
    inverse_1 = columns_of(diag_inverse[1])

    def reduce_cols(partial_sum):
        terms = lax.all_to_all(partial_sum.reshape(n_cols, width, slab), "cols", 0, 0, tiled=True)
        return jnp.sum(terms, axis=0)

    def all_slabs(block):
        spread = jnp.broadcast_to(block[None], (n_rows, width, slab))
        return lax.all_to_all(spread, "rows", 0, 0, tiled=True)

    swap = [
        (r * n_cols + c, (c // 2) * n_cols + 2 * r + c % 2) for r in range(n_rows) for c in range(n_cols)
    ]

    def solution_rows(block):
        piece = lax.ppermute(block, ("rows", "cols"), swap)
        return lax.all_gather(piece, "cols", axis=0, tiled=False)

    def as_rows(pieces):
        pieces = pieces.reshape(n_rows, halves, width, slab).transpose(1, 2, 0, 3)
        return pieces.reshape(block_rows, list_len)

    first = reduce_cols(dot(inverse_0, rhs, ((1,), (0,)), HIGH))
    first_out = solution_rows(first)
    first_all = all_slabs(first)
    second_rhs = reduce_cols(second_gram - dot(below, first, ((1,), (0,)), HIGH))
    second = reduce_cols(dot(inverse_1, second_rhs, ((1,), (0,)), HIGH))
    second_all = all_slabs(second)

    trail_gram = lax.dot_general(
        gram_slots[2:], to_list, (((2,), (0,)), ((), ())), precision=HIGHEST, preferred_element_type=F32
    )
    first_trail = jnp.einsum("trc,scp->trsp", trail_factor[:, 0], first_all, precision=HIGH, preferred_element_type=F32)
    second_trail = jnp.einsum("trc,scp->trsp", trail_factor[:, 1], second_all, precision=HIGH, preferred_element_type=F32)
    terms = trail_gram - first_trail.reshape(trail_gram.shape) - second_trail.reshape(trail_gram.shape)
    trail_out = lax.psum_scatter(terms, "cols", scatter_dimension=2, tiled=True)
    second_piece = lax.ppermute(second, ("rows", "cols"), swap)
    second_out = lax.all_to_all(
        jnp.broadcast_to(second_piece[None], (n_cols, width, slab)), "cols", 0, 0, tiled=True
    )
    return jnp.stack([as_rows(first_out), as_rows(second_out)]), trail_out


def solution(mesh):
    return jax.shard_map(
        body,
        mesh=mesh,
        in_specs=(
            P(),
            P(None, "rows", "cols"),
            P(None, "rows", "cols"),
            P("rows", "cols"),
            P(None, None, "rows", "cols"),
        ),
        out_specs=(P(None, "rows", None), P(None, "rows", "cols")),
        check_vma=False,
    )
```

time: 839 us -> 342 us (0.41)
  waiting for transfers between devices: 724 us -> 152 us
  blocking collectives: 0 us -> 48.8 us
  starting transfers between devices: 7.62 us -> 45.9 us
  other arithmetic: 27.5 us -> 5.22 us
    psum x7 -> x0, waiting for transfers between devices: 508 us -> none  [the longest x4 238 us: from_root(): return lax.psum(kept, axis)]
    all_to_all x1 -> x6, waiting for transfers between devices: 21.5 us -> 111 us  [the longest x2 53.8 us: reduce_cols(): lax.all_to_all(partial_sum.reshape(n_cols, width, slab), 'cols', 0, 0, ti...]
    reduce_scatter x2 -> x1, waiting for transfers between devices: 126 us -> 39.5 us  [body(): trail_out = lax.psum_scatter(terms, 'cols', scatter_dimension=2, tiled=True)]
    all_gather x1 -> x4, waiting for transfers between devices: 68.9 us -> 0.08 us  [the longest x3 0.06 us: columns_of(): return lax.all_gather(block, 'rows', axis=0, tiled=True)]
    all_to_all x0 -> x2, blocking collectives: none -> 48.8 us  [the longest x1 31.3 us: reduce_cols(): lax.all_to_all(partial_sum.reshape(n_cols, width, slab), 'cols', 0, 0, ti...]
    all_to_all x1 -> x6, starting transfers between devices: 7.02 us -> 44 us  [the longest x1 18.3 us: body(): lax.all_to_all(jnp.broadcast_to(second_piece[None], (n_cols, width, slab)...]
    gather x3 -> x0, local copies, waits for them, and re-layouts: 20.5 us -> none  [the longest x1 14.9 us: body(): panel_rhs = jnp.take(whole, owners * capacity + slots_of, axis=2)]
    select_n x7 -> x0, other arithmetic: 13.5 us -> none  [the longest x4 8.01 us: from_root(): jnp.where(lax.axis_index(axis) == source, value, 0).astype(value.dtype)]
  transfers between devices with their start and end apart: 11 -> 13, of which waited for: 11 -> 7; matrix products, arithmetic and copies ran while one was open for 6% -> 21% of each run, Pallas kernels for 0% -> 0%
where the time goes in v1:
time: 342 us; the launch traced here: 341 us
  waiting for transfers between devices  152 us (44%)
  blocking collectives  48.8 us (14%)
  starting transfers between devices  45.9 us (13%)
  matrix products  40.1 us (12%)
  local copies, waits for them, and re-layouts  35.2 us (10%)
  between operations  14 us (4%)
  other arithmetic  5.22 us (2%)
    all_to_all x2, waiting for transfers between devices, reduce_cols(): lax.all_to_all(partial_sum.reshape(n_cols, width, slab), 'cols', 0, 0, ti...  53.8 us
    reduce_scatter x1, waiting for transfers between devices, body(): trail_out = lax.psum_scatter(terms, 'cols', scatter_dimension=2, tiled=True)  39.5 us
    all_to_all x1, blocking collectives, reduce_cols(): lax.all_to_all(partial_sum.reshape(n_cols, width, slab), 'cols', 0, 0, ti...  31.3 us
    all_to_all x1, waiting for transfers between devices, body(): lax.all_to_all(jnp.broadcast_to(second_piece[None], (n_cols, width, slab)...  26.6 us
    all_to_all x2, waiting for transfers between devices, all_slabs(): return lax.all_to_all(spread, 'rows', 0, 0, tiled=True)  22.1 us
    all_to_all x1, starting transfers between devices, body(): lax.all_to_all(jnp.broadcast_to(second_piece[None], (n_cols, width, slab)...  18.3 us
    all_to_all x1, blocking collectives, body(): slab_gram = lax.all_to_all(outgoing, 'rows', 0, 0, tiled=True)  17.5 us
    dot_general x5, matrix products, dot(): lax.dot_general(a, b, (dims, ((), ())), precision=precision, preferred_el...  15.6 us
  transfers between devices with their start and end apart: 13, of which 7 were waited for; matrix products, arithmetic and copies ran while one was open for 21% of the time, Pallas kernels for 0%

profile of v1, /device:TPU:0, one launch (start us, length us, event | category | flops | bytes accessed | tf_op | source)
XLA Modules:
  0.0 341.2 jit_solution(11143026178181830486)
XLA Ops:
  7.2 0.0 all-gather.10.cloned.1.call-start
  7.2 2.2 fusion.53
  9.5 0.0 all-gather.8.cloned.1.call-start
  9.5 0.7 all-gather.8.cloned.1.call-update
  10.2 0.0 all-gather.14.cloned.1.call-start
  10.3 0.7 all-gather.14.cloned.1.call-update
  11.0 0.1 eq.80
  11.1 0.3 convert_reduce_fusion
  11.4 0.1 select_reduce_fusion.1
  11.6 0.1 select_reduce_fusion
  11.7 0.1 reshape.105
  11.7 0.3 fusion.11
  12.0 0.1 reshape.104
  12.1 1.0 convolution_bitcast_fusion.3
  13.0 1.6 fusion.15
  14.7 17.5 %all_to_all.40 = f32[8,16,2,512]{3,1,2,0:T(8,128)S(1)} all-to-all(f32[8,16,2,512]{3,1,2,0:T(8,128)S(1)} %copy.46), channel_id=1, replica_groups=mesh['rows'=8,'cols'=16] {'rows'}, dimensions={0} | all-to-all | bytes 1048576 | tf_op jit(solution)/shard_map/all_to_all | solution.py:64
  32.3 0.2 reshape_squeeze.3
  32.4 0.7 copy.47
  33.2 9.3 %all-to-all-start.1 = ((f32[16,16,256]{2,1,0:T(8,128)}), f32[16,16,256]{2,1,0:T(8,128)S(1)}, u32[]{:S(2)}, u32[]{:S(2)}) async-start(f32[16,16,256]{2,1,0:T(8,128)} %bitcast.5), calls=%async_computation.1 | async-start | bytes 524288 | tf_op jit(solution)/shard_map/all_to_all | solution.py:68
  42.5 0.1 multiply_add_fusion
  42.6 8.4 %all-to-all-done.1 = f32[16,16,256]{2,1,0:T(8,128)S(1)} async-done(((f32[16,16,256]{2,1,0:T(8,128)}), f32[16,16,256]{2,1,0:T(8,128)S(1)}, u32[]{:S(2)}, u32[]{:S(2)}) %all-to-all-start.1) | async-done | bytes 262176 | tf_op jit(solution)/shard_map/all_to_all | solution.py:68
  51.0 0.4 fusion.28
  51.4 4.5 %fusion.3 = f32[128,4096]{1,0:T(8,128)S(1)} fusion(f32[256,128]{1,0:T(8,128)S(1)} %fusion.28, f32[1,4096,256]{2,1,0:T(8,128)} %all-gather.10.cloned.1.call-done), kind=kOutput, calls=%fused_computation.7 | convolution fusion | flops 805306368 | bytes 6422528 | tf_op jit(solution)/shard_map/dot_general | solution.py:13
  55.9 1.6 copy.70
  57.5 4.1 %all-to-all-start.2 = ((f32[16,256,128]{1,2,0:T(8,128)}), f32[16,256,128]{1,2,0:T(8,128)S(1)}, u32[]{:S(2)}, u32[]{:S(2)}) async-start(f32[16,256,128]{1,2,0:T(8,128)} %bitcast.106), calls=%async_computation.2 | async-start | bytes 4194304 | tf_op jit(solution)/shard_map/all_to_all | solution.py:92
  61.6 0.1 broadcast_compare_fusion.1
  61.7 3.1 fusion.37
  64.9 27.7 %all-to-all-done.2 = f32[16,256,128]{1,2,0:T(8,128)S(1)} async-done(((f32[16,256,128]{1,2,0:T(8,128)}), f32[16,256,128]{1,2,0:T(8,128)S(1)}, u32[]{:S(2)}, u32[]{:S(2)}) %all-to-all-start.2) | async-done | bytes 2097184 | tf_op jit(solution)/shard_map/all_to_all | solution.py:92
  92.5 0.1 reduce_sum.67
  92.7 5.3 %fusion = f32[4096,128]{1,0:T(8,128)S(1)} fusion(f32[4096,128]{1,0:T(8,128)} %fusion.37, f32[256,128]{0,1:T(8,128)S(1)} %reduce_sum.67, f32[4096,256]{1,0:T(8,128)} %all-gather.8.cloned.1.call-done), kind=kOutput, calls=%fused_computation.3 | convolution fusion | flops 805830656 | bytes 8519680 | tf_op jit(solution)/shard_map/dot_general | solution.py:13
  98.0 31.3 %all_to_all.41 = f32[16,256,128]{2,1,0:T(8,128)S(1)} all-to-all(f32[16,256,128]{2,1,0:T(8,128)S(1)} %bitcast.108), channel_id=1, replica_groups=mesh['rows'=8,'cols'=16] {'cols'}, dimensions={0} | all-to-all | bytes 4194304 | tf_op jit(solution)/shard_map/all_to_all | solution.py:92
  129.3 0.1 reduce_sum.68
  129.5 4.5 %fusion.1 = f32[128,4096]{1,0:T(8,128)S(1)} fusion(f32[256,128]{1,0:T(8,128)S(1)} %reduce_sum.68, f32[1,4096,256]{2,1,0:T(8,128)} %all-gather.14.cloned.1.call-done), kind=kOutput, calls=%fused_computation.5 | convolution fusion | flops 805306368 | bytes 6422528 | tf_op jit(solution)/shard_map/dot_general | solution.py:13
  133.9 1.5 copy.69
  135.5 3.7 %all-to-all-start.4 = ((f32[16,256,128]{1,2,0:T(8,128)}), f32[16,256,128]{1,2,0:T(8,128)S(1)}, u32[]{:S(2)}, u32[]{:S(2)}) async-start(f32[16,256,128]{1,2,0:T(8,128)} %bitcast.104), calls=%async_computation.4 | async-start | bytes 4194304 | tf_op jit(solution)/shard_map/all_to_all | solution.py:92
  139.2 0.2 all-gather.12.cloned.1.call-start
  139.4 0.7 collective-permute-start
  140.1 0.6 copy-done.2
  140.8 26.1 %all-to-all-done.4 = f32[16,256,128]{1,2,0:T(8,128)S(1)} async-done(((f32[16,256,128]{1,2,0:T(8,128)}), f32[16,256,128]{1,2,0:T(8,128)S(1)}, u32[]{:S(2)}, u32[]{:S(2)}) %all-to-all-start.4) | async-done | bytes 2097184 | tf_op jit(solution)/shard_map/all_to_all | solution.py:92
  166.9 1.1 broadcast_in_dim.38
  168.0 5.0 %all-to-all-start.6 = ((f32[8,256,128]{1,2,0:T(8,128)}), f32[8,256,128]{1,2,0:T(8,128)S(1)}, u32[]{:S(2)}, u32[]{:S(2)}) async-start(f32[8,256,128]{1,2,0:T(8,128)} %broadcast_in_dim.38), calls=%async_computation.6 | async-start | bytes 2097152 | tf_op jit(solution)/shard_map/all_to_all | solution.py:97
  173.0 0.1 reduce_sum.69
  173.1 15.8 %all-to-all-done.6 = f32[8,256,128]{1,2,0:T(8,128)S(1)} async-done(((f32[8,256,128]{1,2,0:T(8,128)}), f32[8,256,128]{1,2,0:T(8,128)S(1)}, u32[]{:S(2)}, u32[]{:S(2)}) %all-to-all-start.6) | async-done | bytes 1048608 | tf_op jit(solution)/shard_map/all_to_all | solution.py:97
  188.9 1.1 broadcast_in_dim.39
  190.0 3.6 %all-to-all-start.7 = ((f32[8,256,128]{1,2,0:T(8,128)}), f32[8,256,128]{1,2,0:T(8,128)S(1)}, u32[]{:S(2)}, u32[]{:S(2)}) async-start(f32[8,256,128]{1,2,0:T(8,128)} %broadcast_in_dim.39), calls=%async_computation.7 | async-start | bytes 2097152 | tf_op jit(solution)/shard_map/all_to_all | solution.py:97
  193.6 0.0 reduce-scatter.2.cloned.1.call-start
  193.6 5.3 %convolution_bitcast_fusion.2 = f32[4,512,8,128]{1,3,0,2:T(8,128)S(1)} fusion(f32[4,2,512,256]{3,2,1,0:T(8,128)} %param.9, f32[8,256,128]{1,2,0:T(8,128)S(1)} %all-to-all-done.6), kind=kOutput, calls=%fused_computation.10 | convolution fusion | flops 3221225472 | bytes 11534336 | tf_op jit(solution)/shard_map/trc,scp->trsp/dot_general | solution.py:121
  198.9 4.2 %copy.56 = f32[4,512,8,128]{1,3,2,0:T(8,128)} copy(f32[4,512,8,128]{1,3,0,2:T(8,128)S(1)} %convolution_bitcast_fusion.2) | data formatting | bytes 16777216 | tf_op jit(solution)/shard_map/trc,scp->trsp/dot_general | solution.py:121
  203.2 6.3 %all-to-all-done.7 = f32[8,256,128]{1,2,0:T(8,128)S(1)} async-done(((f32[8,256,128]{1,2,0:T(8,128)}), f32[8,256,128]{1,2,0:T(8,128)S(1)}, u32[]{:S(2)}, u32[]{:S(2)}) %all-to-all-start.7) | async-done | bytes 1048608 | tf_op jit(solution)/shard_map/all_to_all | solution.py:97
  209.5 5.4 %convolution_bitcast_fusion.1 = f32[4,512,8,128]{1,3,0,2:T(8,128)S(1)} fusion(f32[4,2,512,256]{3,2,1,0:T(8,128)} %param.9, f32[8,256,128]{1,2,0:T(8,128)S(1)} %all-to-all-done.7), kind=kOutput, calls=%fused_computation.9 | convolution fusion | flops 3221225472 | bytes 11534336 | tf_op jit(solution)/shard_map/trc,scp->trsp/dot_general | solution.py:122
  214.9 4.6 %copy.58 = f32[4,512,8,128]{1,3,2,0:T(8,128)} copy(f32[4,512,8,128]{1,3,0,2:T(8,128)S(1)} %convolution_bitcast_fusion.1) | data formatting | bytes 16777216 | tf_op jit(solution)/shard_map/trc,scp->trsp/dot_general | solution.py:122
  219.5 8.8 %bitcast_subtract_fusion = f32[4,512,1024]{1,2,0:T(8,128)} fusion(f32[4,512,8,128]{1,3,2,0:T(8,128)} %copy.58, f32[4,512,8,128]{1,3,2,0:T(8,128)S(1)} %bitcast.101, f32[6,512,128]{2,1,0:T(8,128)S(1)} %copy-done.1, s32[1024]{0:T(1024)S(1)} %get-tuple-element.11, pred[1024]{0:T(1024)(128)(4,1)S(1)} %get-tuple-element.4), kind=kOutput, calls=%fused_computation | convolution fusion | flops 3225681920 | bytes 26219520 | tf_op jit(solution)/shard_map/dot_general | solution.py:118
  228.4 0.9 collective-permute-start.1
  229.3 0.1 copy.53
  229.4 1.5 broadcast_in_dim.37
  230.9 18.3 %all-to-all-start.5 = ((f32[16,256,128]{2,1,0:T(8,128)}), f32[16,256,128]{2,1,0:T(8,128)S(1)}, u32[]{:S(2)}, u32[]{:S(2)}) async-start(f32[16,256,128]{2,1,0:T(8,128)} %broadcast_in_dim.37), calls=%async_computation.5 | async-start | bytes 4194304 | tf_op jit(solution)/shard_map/all_to_all | solution.py:126
  249.2 4.0 %reshape.110 = f32[8,2,256,128]{2,1,0,3:T(2,128)} reshape(f32[4096,128]{0,1:T(8,128)} %all-gather.12.cloned.1.call-done) | data formatting | bytes 4194304 | tf_op jit(solution)/shard_map/reshape | solution.py:108
  253.2 3.1 copy.49
  256.3 2.8 stack_reshape.6
  259.1 26.6 %all-to-all-done.5 = f32[16,256,128]{2,1,0:T(8,128)S(1)} async-done(((f32[16,256,128]{2,1,0:T(8,128)}), f32[16,256,128]{2,1,0:T(8,128)S(1)}, u32[]{:S(2)}, u32[]{:S(2)}) %all-to-all-start.5) | async-done | bytes 2097184 | tf_op jit(solution)/shard_map/all_to_all | solution.py:126
  285.7 2.5 copy.54
  288.2 2.9 stack_reshape.7
  291.1 4.1 %pad_maximum_fusion = f32[2,512,1024]{2,1,0:T(8,128)} fusion(f32[1,512,1024]{2,1,0:T(8,128)} %stack_reshape.7, f32[1,512,1024]{2,1,0:T(8,128)S(1)} %copy-done), kind=kLoop, calls=%fused_computation.4 | loop fusion | flops 1048576 | bytes 8388608 | tf_op jit(solution)/shard_map/stack | solution.py:129
  295.2 39.5 %reduce-scatter.2.cloned.1.call-done = f32[4,512,64]{1,2,0:T(8,128)} async-done(((f32[4,512,1024]{1,2,0:T(8,128)}), f32[4,512,64]{1,2,0:T(8,128)}) %reduce-scatter.2.cloned.1.call-update) | async-done | bytes 524304 | tf_op jit(solution)/shard_map/reduce_scatter | solution.py:124
  (28 shorter events, 0.3 us)
Async XLA Ops:
  7.2 3.8 %copy-start.3 = (s32[1024]{0:T(1024)S(1)}, s32[1024]{0:T(1024)}, u32[]{:S(2)}) copy-start(s32[1024]{0:T(1024)} %param.5) | copy-start | bytes 12292
  7.2 44.2 %all-gather.10.cloned.1.call-start = ((), (), s32[]{:S(2)}) async-start(), calls=%async_computation.11 | async-start | bytes 4718592 | tf_op jit(solution)/shard_map/all_gather | solution.py:85
  9.5 83.2 %all-gather.8.cloned.1.call-start = ((), (), s32[]{:S(2)}) async-start(), calls=%async_computation.9 | async-start | bytes 4718592 | tf_op jit(solution)/shard_map/all_gather | solution.py:85
  10.2 119.2 %all-gather.14.cloned.1.call-start = ((), (), s32[]{:S(2)}) async-start(), calls=%async_computation.13 | async-start | bytes 4718592 | tf_op jit(solution)/shard_map/all_gather | solution.py:85
  33.2 17.8 %all-to-all-start.1 = ((f32[16,16,256]{2,1,0:T(8,128)}), f32[16,16,256]{2,1,0:T(8,128)S(1)}, u32[]{:S(2)}, u32[]{:S(2)}) async-start(f32[16,16,256]{2,1,0:T(8,128)} %bitcast.5), calls=%async_computation.1 | async-start | bytes 524288 | tf_op jit(solution)/shard_map/all_to_all | solution.py:68
  57.5 35.1 %all-to-all-start.2 = ((f32[16,256,128]{1,2,0:T(8,128)}), f32[16,256,128]{1,2,0:T(8,128)S(1)}, u32[]{:S(2)}, u32[]{:S(2)}) async-start(f32[16,256,128]{1,2,0:T(8,128)} %bitcast.106), calls=%async_computation.2 | async-start | bytes 4194304 | tf_op jit(solution)/shard_map/all_to_all | solution.py:92
  135.5 31.4 %all-to-all-start.4 = ((f32[16,256,128]{1,2,0:T(8,128)}), f32[16,256,128]{1,2,0:T(8,128)S(1)}, u32[]{:S(2)}, u32[]{:S(2)}) async-start(f32[16,256,128]{1,2,0:T(8,128)} %bitcast.104), calls=%async_computation.4 | async-start | bytes 4194304 | tf_op jit(solution)/shard_map/all_to_all | solution.py:92
  139.2 110.0 %all-gather.12.cloned.1.call-start = ((), (), s32[]{:S(2)}) async-start(), calls=%async_computation.12 | async-start | bytes 2228224 | tf_op jit(solution)/shard_map/all_gather | solution.py:105
  139.4 0.7 collective-permute-start
  140.1 0.7 copy-start.2
  168.0 21.0 %all-to-all-start.6 = ((f32[8,256,128]{1,2,0:T(8,128)}), f32[8,256,128]{1,2,0:T(8,128)S(1)}, u32[]{:S(2)}, u32[]{:S(2)}) async-start(f32[8,256,128]{1,2,0:T(8,128)} %broadcast_in_dim.38), calls=%async_computation.6 | async-start | bytes 2097152 | tf_op jit(solution)/shard_map/all_to_all | solution.py:97
  190.0 19.5 %all-to-all-start.7 = ((f32[8,256,128]{1,2,0:T(8,128)}), f32[8,256,128]{1,2,0:T(8,128)S(1)}, u32[]{:S(2)}, u32[]{:S(2)}) async-start(f32[8,256,128]{1,2,0:T(8,128)} %broadcast_in_dim.39), calls=%async_computation.7 | async-start | bytes 2097152 | tf_op jit(solution)/shard_map/all_to_all | solution.py:97
  193.6 141.2 %reduce-scatter.2.cloned.1.call-start = ((), (), s32[]{:S(2)}) async-start(), calls=%async_computation.10 | async-start | bytes 8912896 | tf_op jit(solution)/shard_map/reduce_scatter | solution.py:124
  209.5 10.1 %slice-start = ((s8[8388608]{0:T(1024)(128)(4,1)}), s8[4194304]{0:T(1024)(128)(4,1)S(1)}, s32[]{:S(2)}) async-start(s8[8388608]{0:T(1024)(128)(4,1)} %bitcast.100), calls=%async_computation.14 | async-start | bytes 8388608
  214.9 4.6 %slice-start.1 = ((s8[8388608]{0:T(1024)(128)(4,1)}), s8[4194304]{0:T(1024)(128)(4,1)S(1)}, s32[]{:S(2)}) async-start(s8[8388608]{0:T(1024)(128)(4,1)} %bitcast.100), calls=%async_computation.15 | async-start | bytes 8388608
  214.9 4.6 %copy-start.1 = (f32[6,512,128]{2,1,0:T(8,128)S(1)}, f32[6,512,128]{2,1,0:T(8,128)}, u32[]{:S(2)}) copy-start(f32[6,512,128]{2,1,0:T(8,128)} %param.6) | copy-start | bytes 4718596
  228.4 0.9 collective-permute-start.1
  230.9 54.8 %all-to-all-start.5 = ((f32[16,256,128]{2,1,0:T(8,128)}), f32[16,256,128]{2,1,0:T(8,128)S(1)}, u32[]{:S(2)}, u32[]{:S(2)}) async-start(f32[16,256,128]{2,1,0:T(8,128)} %broadcast_in_dim.37), calls=%async_computation.5 | async-start | bytes 4194304 | tf_op jit(solution)/shard_map/all_to_all | solution.py:126
  288.2 2.9 copy-start
Sparse Core Ops, SparseCore 0:
  10.3 37.1 all-gather.9
  49.2 32.8 all-gather.7
  84.3 32.0 all-gather.13
  141.8 70.2 all-gather.11
  228.5 106.2 reduce-scatter.1
